TPU v7x, 256 devices: a whole 4x4x8 slice. The times are simulated.
256 devices in a mesh: layer: 4 (over x), row: 8 (over y, core), col: 8 (over z).
Axes of the slice: x: 4, y: 4, z: 8, core: 2. Of those that a mesh axis runs over, the one named last changes fastest.
Arguments:
- left_values: bfloat16 [8192, 4, 2048], P('row', 'layer', 'col'), may hold values from -22 to 22
- left_pattern: int32 [32, 4, 8], P('row', 'layer', 'col'), may hold values from 0 to 1, as said below
- right_values: bfloat16 [8192, 4, 2048], P(('layer', 'row'), None, 'col'), may hold values from -6 to 6
- right_pattern: int32 [32, 4, 8], P(('layer', 'row'), None, 'col'), may hold values from 0 to 1, as said below
Outputs:
- expanded: bfloat16 [8192, 4, 2048], P('row', 'layer', 'col')
Inputs may be any that keep to these rules, and one draw needn't show every extreme that they name: `left_pattern`: 1 marks a stored tile, 0 an absent one. `right_pattern`: 1 marks a stored tile, 0 an absent one.
All inputs are finite; a program needn't handle non-finite values.
Results may differ from a plain program's by a relative error of at most 0.001.
Values may be sent and summed in bfloat16 or wider, within the bound.
A program may use at most 64 MiB of HBM per device.

v0:
```python
import jax
import jax.numpy as jnp
from jax import lax
from jax.sharding import PartitionSpec as P


def expand_tiles(values, pattern):
    tile_rows, layers, tile_cols = pattern.shape
    tile_size = values.shape[0] // tile_rows
    blocks = values.reshape(tile_rows, tile_size, layers, tile_cols, tile_size)
    blocks = blocks * pattern[:, None, :, :, None].astype(values.dtype)
    return blocks.reshape(values.shape)


def per_device(left_values, left_pattern, right_values, right_pattern):
    left_block = expand_tiles(left_values, left_pattern)
    right_block = expand_tiles(right_values, right_pattern)
    rows_local = left_block.shape[0]
    columns_local = left_block.shape[2]
    left_flat = left_block.reshape(rows_local, columns_local)
    right_rows = lax.all_gather(right_block, "row", axis=0, tiled=True)
    right_mine = lax.all_to_all(right_rows, "layer", split_axis=1, concat_axis=0, tiled=True)
    right_mine = right_mine.reshape(right_mine.shape[0], columns_local)
    product = jnp.dot(
        lax.all_gather(left_flat, ("layer", "col"), axis=1, tiled=True),
        right_mine,
        preferred_element_type=jnp.float32,
    )
    product = product.reshape(rows_local, 1, columns_local)
    squared = product * product
    column = lax.psum(jnp.sum(squared, axis=0, keepdims=True), "row")
    rows_total = rows_local * lax.axis_size("row")
    colmean = column / rows_total
    return (squared / (colmean + 1e-06)).astype(jnp.bfloat16)


def solution(mesh):
    return jax.shard_map(
        per_device,
        mesh=mesh,
        in_specs=(
            P("row", "layer", "col"),
            P("row", "layer", "col"),
            P(("layer", "row"), None, "col"),
            P(("layer", "row"), None, "col"),
        ),
        out_specs=P("row", "layer", "col"),
        check_vma=False,
    )
```

profile of v0, /device:TPU:1, one launch (start us, length us, event | category | flops | bytes accessed | tf_op | source)
XLA Modules:
  0.0 238.1 jit_solution(10458258856644961506)
XLA Ops:
  6.5 0.0 all-gather.5.cloned.1.call-start
  6.5 0.7 convert_bitcast_fusion
  7.2 1.9 copy_multiply_fusion
  9.1 0.0 all-gather.5.cloned.1.call-update
  9.2 0.0 all-gather.3.cloned.1.call-start
  9.2 0.7 convert_bitcast_fusion.1
  9.9 0.1 broadcast_bitcast_fusion
  9.9 2.0 bitcast_multiply_fusion
  12.0 0.0 all-gather.3.cloned.1.call-update
  12.0 36.2 %all-gather.5.cloned.1.call-done = bf16[2048,4,256]{2,0,1:T(8,128)(2,1)} async-done(((bf16[256,4,256]{2,0,1:T(8,128)(2,1)}), bf16[2048,4,256]{2,0,1:T(8,128)(2,1)}) %all-gather.5.cloned.1.call-update) | async-done | bytes 4194320 | tf_op jit(solution)/shard_map/all_gather | solution.py:21
  48.2 62.8 %all_to_all.15 = bf16[2048,4,256]{2,0,1:T(8,128)(2,1)} all-to-all(bf16[2048,4,256]{2,0,1:T(8,128)(2,1)} %all-gather.5.cloned.1.call-done), channel_id=1, replica_groups=mesh['layer'=4,'row'=8,'col'=8] {'layer'}, dimensions={1} | all-to-all | bytes 8388608 | tf_op jit(solution)/shard_map/all_to_all | solution.py:22
  111.0 95.2 %all-gather.3.cloned.1.call-done = bf16[1024,8192]{1,0:T(8,128)(2,1)} async-done(((bf16[1024,256]{1,0:T(8,128)(2,1)}), bf16[1024,8192]{1,0:T(8,128)(2,1)}) %all-gather.3.cloned.1.call-update) | async-done | bytes 16777232 | tf_op jit(solution)/shard_map/all_gather | solution.py:25
  206.1 9.3 %fusion.1 = (f32[256]{0:T(256)S(1)}, f32[1024,256]{1,0:T(8,128)S(1)}) fusion(bf16[1024,8192]{1,0:T(8,128)(2,1)} %all-gather.3.cloned.1.call-done, bf16[8192,256]{1,0:T(8,128)(2,1)} %bitcast.20), kind=kOutput, calls=%fused_computation.9 | convolution fusion | flops 4295491584 | bytes 22021120 | tf_op jit(solution)/shard_map/dot_general | solution.py:24
  215.5 14.9 %psum.7 = f32[1,1,256]{2,1,0:T(1,128)S(1)} all-reduce(f32[1,1,256]{2,1,0:T(1,128)S(1)} %bitcast.23), channel_id=1, replica_groups=mesh['layer'=4,'row'=8,'col'=8] {'row'}, use_global_device_ids=true, to_apply=%region_1.0 | all-reduce | flops 256 | bytes 2048 | tf_op jit(solution)/shard_map/psum | solution.py:31
  230.4 0.9 fusion
  (2 shorter events, 0.0 us)
Async XLA Ops:
  6.5 41.7 %all-gather.5.cloned.1.call-start = ((), (), s32[]{:S(2)}) async-start(), calls=%async_computation.2 | async-start | bytes 4718592 | tf_op jit(solution)/shard_map/all_gather | solution.py:21
  9.2 197.0 %all-gather.3.cloned.1.call-start = ((), (), s32[]{:S(2)}) async-start(), calls=%async_computation.1 | async-start | bytes 17301504 | tf_op jit(solution)/shard_map/all_gather | solution.py:25
Sparse Core Ops, SparseCore 0:
  9.3 38.8 all-gather.4
  50.7 155.4 all-gather.2
where the time goes:
time: 238 us
  waiting for transfers between devices  131 us (55%)
  blocking collectives  77.7 us (33%)
  between operations  13.4 us (6%)
  matrix products  9.32 us (4%)
  other arithmetic  6.17 us (3%)
    all_gather x1, waiting for transfers between devices, per_device(): lax.all_gather(left_flat, ('layer', 'col'), axis=1, tiled=True)  95.2 us
    all_to_all x1, blocking collectives, per_device(): lax.all_to_all(right_rows, 'layer', split_axis=1, concat_axis=0, tiled=True)  62.8 us
    all_gather x1, waiting for transfers between devices, per_device(): right_rows = lax.all_gather(right_block, 'row', axis=0, tiled=True)  36.2 us
    psum x1, blocking collectives, per_device(): column = lax.psum(jnp.sum(squared, axis=0, keepdims=True), 'row')  14.9 us
    dot_general x1, matrix products, per_device(): jnp.dot(lax.all_gather(left_flat, ('layer', 'col'), axis=1, tiled=True),...  9.32 us
  transfers between devices with their start and end apart: 2, of which 2 were waited for; matrix products, arithmetic and copies ran while one was open for 1% of the time, Pallas kernels for 0%

commit v1 on v0

--- a/solution.py
+++ b/solution.py
@@ -18,14 +18,15 @@
     rows_local = left_block.shape[0]
     columns_local = left_block.shape[2]
     left_flat = left_block.reshape(rows_local, columns_local)
-    right_rows = lax.all_gather(right_block, "row", axis=0, tiled=True)
-    right_mine = lax.all_to_all(right_rows, "layer", split_axis=1, concat_axis=0, tiled=True)
-    right_mine = right_mine.reshape(right_mine.shape[0], columns_local)
-    product = jnp.dot(
-        lax.all_gather(left_flat, ("layer", "col"), axis=1, tiled=True),
-        right_mine,
-        preferred_element_type=jnp.float32,
+    right_flat = right_block.reshape(right_block.shape[0], -1)
+    right_all = lax.all_gather(right_flat, "row", axis=0, tiled=True)
+    left_all = lax.all_gather(left_flat, "col", axis=1, tiled=True)
+    partial = jnp.dot(left_all, right_all, preferred_element_type=jnp.float32)
+    layers = lax.axis_size("layer")
+    partial = jnp.stack(
+        [partial[:, columns_local * l : columns_local * (l + 1)] for l in range(layers)], axis=0
     )
+    product = lax.psum_scatter(partial, "layer", scatter_dimension=0, tiled=True)
     product = product.reshape(rows_local, 1, columns_local)
     squared = product * product
     column = lax.psum(jnp.sum(squared, axis=0, keepdims=True), "row")

time: 238 us -> 194 us (0.82)
  blocking collectives: 77.7 us -> 12.4 us
  waiting for transfers between devices: 131 us -> 148 us
  other arithmetic: 6.17 us -> 10.4 us
    all_to_all x1 -> x0, blocking collectives: 62.8 us -> none  [per_device(): lax.all_to_all(right_rows, 'layer', split_axis=1, concat_axis=0, tiled=True)]
    reduce_scatter x0 -> x1, waiting for transfers between devices: none -> 49.1 us  [per_device(): lax.psum_scatter(partial, 'layer', scatter_dimension=0, tiled=True)]
    all_gather x2, waiting for transfers between devices: 131 us -> 98.9 us  [the longest x1 60.6 us: per_device(): left_all = lax.all_gather(left_flat, 'col', axis=1, tiled=True)]
    psum x1, blocking collectives: 14.9 us -> 12.4 us  [per_device(): column = lax.psum(jnp.sum(squared, axis=0, keepdims=True), 'row')]
  transfers between devices with their start and end apart: 2 -> 3, of which waited for: 2 -> 3; matrix products, arithmetic and copies ran while one was open for 1% -> 2% of each run, Pallas kernels for 0% -> 0%
where the time goes in v1:
time: 194 us; the launch traced here: 193 us
  waiting for transfers between devices  148 us (76%)
  between operations  13.1 us (7%)
  blocking collectives  12.4 us (6%)
  other arithmetic  10.4 us (5%)
  matrix products  7.49 us (4%)
    all_gather x1, waiting for transfers between devices, per_device(): left_all = lax.all_gather(left_flat, 'col', axis=1, tiled=True)  60.6 us
    reduce_scatter x1, waiting for transfers between devices, per_device(): lax.psum_scatter(partial, 'layer', scatter_dimension=0, tiled=True)  49.1 us
    all_gather x1, waiting for transfers between devices, per_device(): right_all = lax.all_gather(right_flat, 'row', axis=0, tiled=True)  38.3 us
    psum x1, blocking collectives, per_device(): column = lax.psum(jnp.sum(squared, axis=0, keepdims=True), 'row')  12.4 us
    dot_general x1, matrix products, per_device(): partial = jnp.dot(left_all, right_all, preferred_element_type=jnp.float32)  7.49 us
  transfers between devices with their start and end apart: 3, of which 3 were waited for; matrix products, arithmetic and copies ran while one was open for 2% of the time, Pallas kernels for 0%

profile of v1, /device:TPU:1, one launch (start us, length us, event | category | flops | bytes accessed | tf_op | source)
XLA Modules:
  0.0 193.0 jit_solution(14705510479955236059)
XLA Ops:
  6.5 0.0 all-gather.3.cloned.1.call-start
  6.5 0.7 convert_bitcast_fusion.1
  7.2 0.1 broadcast_bitcast_fusion
  7.3 2.0 %bitcast_multiply_fusion = bf16[1024,256]{1,0:T(8,128)(2,1)} fusion(bf16[1024,1,256]{2,0,1:T(8,128)(2,1)} %param.4, bf16[1024]{0:T(1024)(128)(2,1)S(1)} %bitcast.29), kind=kLoop, calls=%fused_computation.8 | loop fusion | flops 262144 | bytes 1050624 | tf_op jit(solution)/shard_map/mul | solution.py:11
  9.3 0.0 all-gather.3.cloned.1.call-update
  9.3 0.0 all-gather.5.cloned.1.call-start
  9.4 0.7 convert_bitcast_fusion
  10.1 1.3 broadcast_multiply_fusion
  11.4 0.9 copy.6
  12.3 0.0 all-gather.5.cloned.1.call-update
  12.4 0.0 reduce-scatter.2.cloned.1.call-start
  12.4 60.6 %all-gather.3.cloned.1.call-done = bf16[1024,2048]{1,0:T(8,128)(2,1)} async-done(((bf16[1024,256]{1,0:T(8,128)(2,1)}), bf16[1024,2048]{1,0:T(8,128)(2,1)}) %all-gather.3.cloned.1.call-update) | async-done | bytes 4194320 | tf_op jit(solution)/shard_map/all_gather | solution.py:23
  73.0 38.3 %all-gather.5.cloned.1.call-done = bf16[2048,1024]{1,0:T(8,128)(2,1)} async-done(((bf16[256,1024]{1,0:T(8,128)(2,1)}), bf16[2048,1024]{1,0:T(8,128)(2,1)}) %all-gather.5.cloned.1.call-update) | async-done | bytes 4194320 | tf_op jit(solution)/shard_map/all_gather | solution.py:22
  111.3 7.5 %fusion.1 = f32[1024,1024]{1,0:T(8,128)S(1)} fusion(bf16[1024,2048]{1,0:T(8,128)(2,1)} %all-gather.3.cloned.1.call-done, bf16[2048,1024]{1,0:T(8,128)(2,1)} %all-gather.5.cloned.1.call-done), kind=kOutput, calls=%fused_computation.14 | convolution fusion | flops 4294967296 | bytes 12582912 | tf_op jit(solution)/shard_map/dot_general | solution.py:24
  118.8 0.4 slice_bitcast_fusion.3
  119.2 2.2 %pad_maximum_fusion = f32[4,1024,256]{2,1,0:T(8,128)} fusion(f32[1,1024,256]{2,1,0:T(8,128)S(1)} %get-tuple-element.6, f32[1,1024,256]{2,1,0:T(8,128)S(1)} %get-tuple-element.7, f32[1,1024,256]{2,1,0:T(8,128)S(1)} %get-tuple-element.8, f32[1,1024,256]{2,1,0:T(8,128)S(1)} %get-tuple-element.5), kind=kLoop, calls=%fused_computation | loop fusion | flops 3145728 | bytes 8388608 | tf_op jit(solution)/shard_map/stack | solution.py:26
  121.4 0.0 reduce-scatter.2.cloned.1.call-update
  121.4 49.1 %reduce-scatter.2.cloned.1.call-done = f32[1,1024,256]{2,1,0:T(8,128)} async-done(((f32[4,1024,256]{2,1,0:T(8,128)}), f32[1,1024,256]{2,1,0:T(8,128)}) %reduce-scatter.2.cloned.1.call-update) | async-done | bytes 1048592 | tf_op jit(solution)/shard_map/reduce_scatter | solution.py:29
  170.5 1.4 multiply_reduce_fusion
  171.9 12.4 %psum.7 = f32[1,1,256]{2,1,0:T(1,128)S(1)} all-reduce(f32[1,1,256]{2,1,0:T(1,128)S(1)} %bitcast.30), channel_id=1, replica_groups=mesh['layer'=4,'row'=8,'col'=8] {'row'}, use_global_device_ids=true, to_apply=%region_2.0 | all-reduce | flops 256 | bytes 2048 | tf_op jit(solution)/shard_map/psum | solution.py:32
  184.3 2.1 %fusion = bf16[1024,1,256]{2,0,1:T(8,128)(2,1)} fusion(f32[1,1024,256]{2,1,0:T(8,128)} %reduce-scatter.2.cloned.1.call-done, f32[256]{0:T(256)S(1)} %bitcast.31), kind=kLoop, calls=%fused_computation.6 | loop fusion | flops 786432 | bytes 1573888 | tf_op jit(solution)/shard_map/convert_element_type | solution.py:35
  (2 shorter events, 0.0 us)
Async XLA Ops:
  6.5 66.5 %all-gather.3.cloned.1.call-start = ((), (), s32[]{:S(2)}) async-start(), calls=%async_computation.1 | async-start | bytes 4718592 | tf_op jit(solution)/shard_map/all_gather | solution.py:23
  9.3 102.0 %all-gather.5.cloned.1.call-start = ((), (), s32[]{:S(2)}) async-start(), calls=%async_computation.2 | async-start | bytes 4718592 | tf_op jit(solution)/shard_map/all_gather | solution.py:22
  12.4 158.2 %reduce-scatter.2.cloned.1.call-start = ((), (), s32[]{:S(2)}) async-start(), calls=%async_computation.3 | async-start | bytes 5242880 | tf_op jit(solution)/shard_map/reduce_scatter | solution.py:29
Sparse Core Ops, SparseCore 0:
  9.5 63.5 all-gather.2
  74.9 36.4 all-gather.4
  121.6 48.9 reduce-scatter.1

commit v2 on v0

v2 whole, which is shorter than its diff:
```python
import functools

import jax
import jax.numpy as jnp
from jax import lax
from jax.experimental import pallas as pl
from jax.experimental.pallas import tpu as pltpu
from jax.sharding import PartitionSpec as P

MESH = pl.DeviceIdType.MESH
CHUNKS = 8
GROUPS = 2


def kernel(nl, nr, nz, lp, rp, lv, rv, out, lbuf, rbuf, part, recv_a, recv_b, recv_c, sq, sums, sums_all,
           zl_send, zl_recv, zs_send, zs_recv, y_send, y_recv, s_send, s_recv,
           a_send, a_recv, b_send, b_recv, c_send, c_recv, n_send, n_recv):
    x, r, z = lax.axis_index("layer"), lax.axis_index("row"), lax.axis_index("col")
    core = lax.rem(r, 2)
    sign = 1 - 2 * core
    tile = rv.shape[0]
    rows = lv.shape[0]
    cr = rows // CHUNKS
    gw = tile // GROUPS
    half = tile // 2

    def at_z(v):
        return lax.rem(v + 2 * nz, nz)

    def at_x(v):
        return lax.rem(v + 2 * nl, nl)

    def at_r(v):
        return lax.rem(v + 2 * nr, nr)

    sibling = r + sign
    barrier = pltpu.get_barrier_semaphore()
    peers = [(at_x(x + 1), r, z), (at_x(x - 1), r, z), (x, r, at_z(z + 1)), (x, r, at_z(z - 1))]
    peers += [(x, at_r(r + i), z) for i in range(1, nr)]
    for peer in peers:
        pl.semaphore_signal(barrier, inc=1, device_id=peer, device_id_type=MESH)

    for i in range(rows // tile):
        block = lv[pl.ds(i * tile, tile), :].astype(jnp.float32) * lp[i].astype(jnp.float32)
        lbuf[z, pl.ds(i * tile, tile), :] = block.astype(lbuf.dtype)
    for l in range(nl):
        block = (rv[:, l, :].astype(jnp.float32) * rp[l].astype(jnp.float32)).astype(rbuf.dtype)
        for g in range(GROUPS):
            rbuf[r, g, :, gw * l : gw * (l + 1)] = block[:, gw * g : gw * (g + 1)]
    pl.semaphore_wait(barrier, len(peers))

    def z_copy(h, c, long, receiving):
        d = sign if long else -sign
        owner = at_z(z - d * h) if receiving else at_z(z - d * (h - 1))
        ref = lbuf.at[owner, pl.ds(pl.multiple_of(c * cr, cr), cr), :]
        send, recv = (zl_send, zl_recv) if long else (zs_send, zs_recv)
        return pltpu.make_async_remote_copy(
            src_ref=ref, dst_ref=ref, send_sem=send.at[h - 1, c], recv_sem=recv.at[h - 1, c],
            device_id=(x, r, at_z(z + d)), device_id_type=MESH)

    def z_hop(h, c):
        if h > 1:
            z_copy(h - 1, c, True, True).wait_recv()
        if h <= nz // 2:
            z_copy(h, c, True, False).start()
        if h > 1 and h <= nz // 2:
            z_copy(h - 1, c, False, True).wait_recv()
        if h < nz // 2:
            z_copy(h, c, False, False).start()

    def z_step(t):
        for h in range(1, nz // 2 + 2):
            c = t - (h - 1)
            if isinstance(t, int):
                if 0 <= c < CHUNKS:
                    z_hop(h, c)
            else:
                pl.when(c < CHUNKS)(functools.partial(z_hop, h, c))

    def y_copy(g, i, up, hop, receiving):
        d = 2 if up else -2
        owner = at_r(r - d * hop) if receiving else at_r(r - d * (hop - 1))
        ref = rbuf.at[owner, g, pl.ds(half * i, half), :]
        n = 2 if hop == 2 else (0 if up else 1)
        return pltpu.make_async_remote_copy(
            src_ref=ref, dst_ref=ref, send_sem=y_send.at[g, i, n], recv_sem=y_recv.at[g, i, n],
            device_id=(x, at_r(r + d), z), device_id_type=MESH)

    def s_copy(g, i, n, owner):
        ref = rbuf.at[owner, g, pl.ds(half * i, half), :]
        return pltpu.make_async_remote_copy(
            src_ref=ref, dst_ref=ref, send_sem=s_send.at[g, i, n], recv_sem=s_recv.at[g, i, n],
            device_id=(x, sibling, z), device_id_type=MESH)

    def y_own(g):
        y_copy(g, 0, True, 1, False).start()
        y_copy(g, 1, False, 1, False).start()
        y_copy(g, 1, True, 1, False).start()
        y_copy(g, 0, False, 1, False).start()
        s_copy(g, 0, 3, r).start()
        s_copy(g, 1, 3, r).start()

    def y_first(g):
        for i in (0, 1):
            up = i == 0
            y_copy(g, i, up, 1, True).wait_recv()
            y_copy(g, i, up, 2, False).start()
            s_copy(g, i, 0 if up else 1, at_r(r - 2 if up else r + 2)).start()

    def y_second(g):
        for i in (1, 0):
            up = i == 1
            y_copy(g, i, up, 1, True).wait_recv()
            s_copy(g, i, 0 if up else 1, at_r(r - 2 if up else r + 2)).start()

    def y_third(g):
        for i in (0, 1):
            y_copy(g, i, i == 0, 2, True).wait_recv()
            s_copy(g, i, 2, at_r(r + 4)).start()

    def y_ready(g):
        for i in (0, 1):
            for n, o in ((3, 0), (0, -2), (1, 2), (2, 4)):
                s_copy(g, i, n, at_r(sibling + o)).wait_recv()

    def cell(w):
        first = 1 - lax.min(w // 6, 1)
        c = first * lax.rem(w, 3) + (1 - first) * (w // 2)
        g = first * (w // 3) + (1 - first) * lax.rem(w, 2)
        return g, pl.ds(pl.multiple_of(c * cr, cr), cr)

    def a_copy(w):
        g, rs = cell(w)
        return pltpu.make_async_remote_copy(
            src_ref=part.at[at_x(x + 2), g, rs, :], dst_ref=recv_a.at[g, rs, :], send_sem=a_send.at[w],
            recv_sem=a_recv.at[w], device_id=(at_x(x + sign), r, z), device_id_type=MESH)

    def c_copy(w):
        g, rs = cell(w)
        return pltpu.make_async_remote_copy(
            src_ref=part.at[at_x(x - sign), g, rs, :], dst_ref=recv_c.at[g, rs, :], send_sem=c_send.at[w],
            recv_sem=c_recv.at[w], device_id=(at_x(x - sign), r, z), device_id_type=MESH)

    def b_copy(w):
        g, rs = cell(w)
        return pltpu.make_async_remote_copy(
            src_ref=part.at[at_x(x + sign), g, rs, :], dst_ref=recv_b.at[g, rs, :], send_sem=b_send.at[w],
            recv_sem=b_recv.at[w], device_id=(at_x(x + sign), r, z), device_id_type=MESH)

    items = CHUNKS * GROUPS

    def multiply(w):
        g, rs = cell(w)
        acc = jnp.dot(lbuf[0, rs, :], rbuf[0, g], preferred_element_type=jnp.float32)
        for j in range(1, nz):
            acc += jnp.dot(lbuf[j, rs, :], rbuf[j, g], preferred_element_type=jnp.float32)
        for l in range(nl):
            part[l, g, rs, :] = acc[:, gw * l : gw * (l + 1)]

    def add_first(w):
        g, rs = cell(w)
        a_copy(w).wait_recv()
        part[at_x(x + sign), g, rs, :] += recv_a[g, rs, :]

    def finish(w):
        g, rs = cell(w)
        c_copy(w).wait_recv()
        b_copy(w).wait_recv()
        total = part[x, g, rs, :] + recv_c[g, rs, :] + recv_b[g, rs, :]
        square = total * total
        sq[g, rs, :] = square
        sums[g] += jnp.sum(square.reshape(cr // 8, 8, gw), axis=0)

    sums[...] = jnp.zeros_like(sums)
    z_step(0)
    y_own(0)
    y_own(1)
    z_step(1)
    z_step(2)
    y_first(0)
    y_second(0)
    z_step(3)
    y_third(0)
    y_ready(0)

    def body(w, _):
        for w0, t in ((0, 4), (1, 5), (2, 6), (5, 7)):
            pl.when(w == w0)(functools.partial(z_step, t))

        @pl.when((w == 0))
        def _():
            y_first(1)

        @pl.when((w == 1))
        def _():
            y_second(1)
            y_third(1)

        @pl.when((w == 3))
        def _():
            y_ready(1)

        @pl.when((w >= 8) & (lax.rem(w, 2) == 0) & (w < items))
        def _():
            z_step(w // 2 + 4)

        @pl.when((w >= 2) & (w < items + 2))
        def _():
            add_first(w - 2)

        @pl.when(w < items)
        def _():
            multiply(w)

        @pl.when((w >= 2) & (w < items + 2))
        def _():
            b_copy(w - 2).start()

        @pl.when(w < items)
        def _():
            a_copy(w).start()
            c_copy(w).start()

        @pl.when(w >= 4)
        def _():
            finish(w - 4)

        return 0

    lax.fori_loop(0, items + 4, body, 0)

    def n_copy(i, receiving):
        slot = at_r(r - i) if receiving else r
        ref = sums_all.at[slot]
        return pltpu.make_async_remote_copy(
            src_ref=ref, dst_ref=ref, send_sem=n_send.at[i], recv_sem=n_recv.at[i],
            device_id=(x, at_r(r + i), z), device_id_type=MESH)

    sums_all[r] = sums[...]
    for i in range(1, nr):
        n_copy(i, False).start()

    def drain(w, _):
        a_copy(w).wait_send()
        b_copy(w).wait_send()
        c_copy(w).wait_send()
        return 0

    lax.fori_loop(0, items, drain, 0)

    def drain_z(c, _):
        for h in range(1, nz // 2 + 1):
            z_copy(h, c, True, False).wait_send()
            if h < nz // 2:
                z_copy(h, c, False, False).wait_send()
        return 0

    lax.fori_loop(0, CHUNKS, drain_z, 0)
    for g in range(GROUPS):
        for i in (0, 1):
            for up in (True, False):
                y_copy(g, i, up, 1, False).wait_send()
            y_copy(g, i, i == 0, 2, False).wait_send()
            for n in range(4):
                s_copy(g, i, n, r).wait_send()

    for i in range(1, nr):
        n_copy(i, True).wait_recv()
    total = sums_all[0]
    for i in range(1, nr):
        total += sums_all[i]
    scale = 1.0 / (jnp.sum(total, axis=1, keepdims=True) * (1.0 / (rows * nr)) + 1e-6)
    for g in range(GROUPS):
        out[:, gw * g : gw * (g + 1)] = (sq[g] * scale[g]).astype(out.dtype)
    for i in range(1, nr):
        n_copy(i, False).wait_send()


def per_device(nl, nr, nz, left_values, left_pattern, right_values, right_pattern):
    rows, _, tile = left_values.shape
    f32, bf16 = jnp.float32, jnp.bfloat16
    gw = tile // GROUPS
    items = CHUNKS * GROUPS
    dma = pltpu.SemaphoreType.DMA
    smem, vmem = pl.BlockSpec(memory_space=pltpu.SMEM), pl.BlockSpec(memory_space=pltpu.VMEM)
    out = pl.pallas_call(
        functools.partial(kernel, nl, nr, nz),
        out_shape=jax.ShapeDtypeStruct((rows, tile), bf16),
        in_specs=[smem, smem, vmem, vmem],
        out_specs=vmem,
        scratch_shapes=[
            pltpu.VMEM((nz, rows, tile), bf16),
            pltpu.VMEM((nr, GROUPS, tile, nl * gw), bf16),
            pltpu.VMEM((nl, GROUPS, rows, gw), f32),
            pltpu.VMEM((GROUPS, rows, gw), f32),
            pltpu.VMEM((GROUPS, rows, gw), f32),
            pltpu.VMEM((GROUPS, rows, gw), f32),
            pltpu.VMEM((GROUPS, rows, gw), f32),
            pltpu.VMEM((GROUPS, 8, gw), f32),
            pltpu.VMEM((nr, GROUPS, 8, gw), f32),
            dma((nz // 2, CHUNKS)), dma((nz // 2, CHUNKS)),
            dma((nz // 2, CHUNKS)), dma((nz // 2, CHUNKS)),
            dma((GROUPS, 2, 3)), dma((GROUPS, 2, 3)),
            dma((GROUPS, 2, 4)), dma((GROUPS, 2, 4)),
            dma((items,)), dma((items,)), dma((items,)), dma((items,)), dma((items,)), dma((items,)),
            dma((nr,)), dma((nr,)),
        ],
        compiler_params=pltpu.CompilerParams(
            collective_id=0, has_side_effects=True, vmem_limit_bytes=40 * 1024 * 1024),
    )(left_pattern.reshape(-1), right_pattern.reshape(-1), left_values.reshape(rows, tile), right_values)
    return out.reshape(rows, 1, tile)


def solution(mesh):
    sizes = mesh.shape["layer"], mesh.shape["row"], mesh.shape["col"]
    return jax.shard_map(
        functools.partial(per_device, *sizes),
        mesh=mesh,
        in_specs=(
            P("row", "layer", "col"),
            P("row", "layer", "col"),
            P(("layer", "row"), None, "col"),
            P(("layer", "row"), None, "col"),
        ),
        out_specs=P("row", "layer", "col"),
        check_vma=False,
    )
```

time: 238 us -> 91 us (0.38)
  waiting for transfers between devices: 131 us -> 0 us
  Pallas kernels: 0 us -> 87.2 us
  blocking collectives: 77.7 us -> 0 us
  between operations: 13.4 us -> 0.01 us
  matrix products: 9.32 us -> 0 us
  other arithmetic: 6.17 us -> 0 us
  local copies, waits for them, and re-layouts: 0.08 us -> 3.55 us
    all_gather x2 -> x0, waiting for transfers between devices: 131 us -> none  [the longest x1 95.2 us: per_device(): lax.all_gather(left_flat, ('layer', 'col'), axis=1, tiled=True)]
    pallas_call x0 -> x1, Pallas kernels: none -> 87.2 us  [per_device(): pl.pallas_call(functools.partial(kernel, nl, nr, nz), out_shape=jax.Shape...]
    all_to_all x1 -> x0, blocking collectives: 62.8 us -> none  [per_device(): lax.all_to_all(right_rows, 'layer', split_axis=1, concat_axis=0, tiled=True)]
    psum x1 -> x0, blocking collectives: 14.9 us -> none  [per_device(): column = lax.psum(jnp.sum(squared, axis=0, keepdims=True), 'row')]
    dot_general x1 -> x0, matrix products: 9.32 us -> none  [per_device(): jnp.dot(lax.all_gather(left_flat, ('layer', 'col'), axis=1, tiled=True),...]
    mul x2 -> x0, other arithmetic: 3.97 us -> none  [expand_tiles(): blocks = blocks * pattern[:, None, :, :, None].astype(values.dtype)]
    unnamed x2 -> x9, local copies, waits for them, and re-layouts: 0.08 us -> 3.55 us
  transfers between devices with their start and end apart: 2 -> 0, of which waited for: 2 -> 0; matrix products, arithmetic and copies ran while one was open for 1% -> 0% of each run, Pallas kernels for 0% -> 0%
where the time goes in v2:
time: 91 us; the launch traced here: 90.8 us
  Pallas kernels  87.2 us (96%)
  local copies, waits for them, and re-layouts  3.55 us (4%)
    pallas_call x1, Pallas kernels, per_device(): pl.pallas_call(functools.partial(kernel, nl, nr, nz), out_shape=jax.Shape...  87.2 us
    unnamed x9, local copies, waits for them, and re-layouts  3.55 us

profile of v2, /device:TPU:1, one launch (start us, length us, event | category | flops | bytes accessed | tf_op | source)
XLA Modules:
  0.0 90.8 jit_solution(14611498461812548424)
XLA Ops:
  0.0 0.0 copy-start.2
  0.0 0.0 copy-start.3
  0.0 0.7 copy-done.2
  0.7 0.0 copy-done.3
  0.7 0.0 copy-start
  0.7 1.0 %copy-done = bf16[1024,1,256]{2,0,1:T(8,128)(2,1)S(1)} copy-done((bf16[1024,1,256]{2,0,1:T(8,128)(2,1)S(1)}, bf16[1024,1,256]{2,0,1:T(8,128)(2,1)}, u32[]{:S(2)}) %copy-start) | copy-done | bytes 524312
  1.7 0.0 copy-start.1
  1.7 1.0 %copy-done.1 = bf16[256,4,256]{2,1,0:T(4,128)(2,1)S(1)} copy-done((bf16[256,4,256]{2,1,0:T(4,128)(2,1)S(1)}, bf16[256,4,256]{2,1,0:T(4,128)(2,1)}, u32[]{:S(2)}) %copy-start.1) | copy-done | bytes 524312
  2.8 87.2 %shard_map.46 = bf16[1024,256]{1,0:T(8,128)(2,1)S(1)} custom-call(s32[4]{0:T(128)S(1)} %bitcast.6, s32[4]{0:T(128)S(1)} %bitcast.7, bf16[1024,256]{1,0:T(8,128)(2,1)S(1)} %bitcast.5, bf16[256,4,256]{2,1,0:T(4,128)(2,1)S(1)} %copy-done.1), custom_call_target="tpu_custom_call" | custom-call | tf_op jit(solution)/shard_map/pallas_call | solution.py:286
  90.0 0.8 copy.6
Async XLA Ops:
  0.0 0.7 copy-start.2
  0.0 0.7 copy-start.3
  0.7 1.0 %copy-start = (bf16[1024,1,256]{2,0,1:T(8,128)(2,1)S(1)}, bf16[1024,1,256]{2,0,1:T(8,128)(2,1)}, u32[]{:S(2)}) copy-start(bf16[1024,1,256]{2,0,1:T(8,128)(2,1)} %param.4) | copy-start | bytes 1572868
  1.7 1.0 %copy-start.1 = (bf16[256,4,256]{2,1,0:T(4,128)(2,1)S(1)}, bf16[256,4,256]{2,1,0:T(4,128)(2,1)}, u32[]{:S(2)}) copy-start(bf16[256,4,256]{2,1,0:T(4,128)(2,1)} %rv.1) | copy-start | bytes 1572868

commit v3 on v2

--- a/solution.py
+++ b/solution.py
@@ -8,13 +8,15 @@
 from jax.sharding import PartitionSpec as P
 
 MESH = pl.DeviceIdType.MESH
-CHUNKS = 8
+CHUNKS = 16
+LEAD = 1
+LAG = 4
 GROUPS = 2
 
 
-def kernel(nl, nr, nz, lp, rp, lv, rv, out, lbuf, rbuf, part, recv_a, recv_b, recv_c, sq, sums, sums_all,
+def kernel(nl, nr, nz, lp, rp, lv_hbm, rv_hbm, out, lv, rv, lbuf, rbuf, part, recv_a, recv_b, recv_c, sq, sums, sums_all,
            zl_send, zl_recv, zs_send, zs_recv, y_send, y_recv, s_send, s_recv,
-           a_send, a_recv, b_send, b_recv, c_send, c_recv, n_send, n_recv):
+           a_send, a_recv, b_send, b_recv, c_send, c_recv, n_send, n_recv, in_sem):
     x, r, z = lax.axis_index("layer"), lax.axis_index("row"), lax.axis_index("col")
     core = lax.rem(r, 2)
     sign = 1 - 2 * core
@@ -37,12 +39,18 @@
     barrier = pltpu.get_barrier_semaphore()
     peers = [(at_x(x + 1), r, z), (at_x(x - 1), r, z), (x, r, at_z(z + 1)), (x, r, at_z(z - 1))]
     peers += [(x, at_r(r + i), z) for i in range(1, nr)]
+    fetch_left = pltpu.make_async_copy(lv_hbm, lv, in_sem.at[0])
+    fetch_right = pltpu.make_async_copy(rv_hbm, rv, in_sem.at[1])
+    fetch_left.start()
+    fetch_right.start()
     for peer in peers:
         pl.semaphore_signal(barrier, inc=1, device_id=peer, device_id_type=MESH)
 
+    fetch_left.wait()
     for i in range(rows // tile):
         block = lv[pl.ds(i * tile, tile), :].astype(jnp.float32) * lp[i].astype(jnp.float32)
         lbuf[z, pl.ds(i * tile, tile), :] = block.astype(lbuf.dtype)
+    fetch_right.wait()
     for l in range(nl):
         block = (rv[:, l, :].astype(jnp.float32) * rp[l].astype(jnp.float32)).astype(rbuf.dtype)
         for g in range(GROUPS):
@@ -68,13 +76,17 @@
         if h < nz // 2:
             z_copy(h, c, False, False).start()
 
-    def z_step(t):
-        for h in range(1, nz // 2 + 2):
-            c = t - (h - 1)
-            if isinstance(t, int):
+    def z_tick(n, odd):
+        for h in range(nz // 2 + 1, 0, -1):
+            delay = 3 * (h - 1) if h > 1 else -2 * LEAD
+            if delay % 2 != odd:
+                continue
+            if isinstance(n, int):
+                c = (n - delay) // 2
                 if 0 <= c < CHUNKS:
                     z_hop(h, c)
             else:
+                c = (n - delay) // 2
                 pl.when(c < CHUNKS)(functools.partial(z_hop, h, c))
 
     def y_copy(g, i, up, hop, receiving):
@@ -106,6 +118,8 @@
             y_copy(g, i, up, 1, True).wait_recv()
             y_copy(g, i, up, 2, False).start()
             s_copy(g, i, 0 if up else 1, at_r(r - 2 if up else r + 2)).start()
+        if g + 1 < GROUPS:
+            y_own(g + 1)
 
     def y_second(g):
         for i in (1, 0):
@@ -124,9 +138,11 @@
                 s_copy(g, i, n, at_r(sibling + o)).wait_recv()
 
     def cell(w):
-        first = 1 - lax.min(w // 6, 1)
-        c = first * lax.rem(w, 3) + (1 - first) * (w // 2)
-        g = first * (w // 3) + (1 - first) * lax.rem(w, 2)
+        late = lax.min(w // 5, 1)
+        q, s = lax.max(w - 5, 0) // 5, lax.rem(w, 5)
+        odd = lax.rem(s, 2)
+        c = (1 - late) * w + late * (odd * (5 + 2 * q) + (1 - odd) * 3 * q + s // 2)
+        g = late * (1 - odd)
         return g, pl.ds(pl.multiple_of(c * cr, cr), cr)
 
     def a_copy(w):
@@ -171,63 +187,56 @@
         sq[g, rs, :] = square
         sums[g] += jnp.sum(square.reshape(cr // 8, 8, gw), axis=0)
 
-    sums[...] = jnp.zeros_like(sums)
-    z_step(0)
-    y_own(0)
-    y_own(1)
-    z_step(1)
-    z_step(2)
-    y_first(0)
-    y_second(0)
-    z_step(3)
-    y_third(0)
-    y_ready(0)
-
-    def body(w, _):
-        for w0, t in ((0, 4), (1, 5), (2, 6), (5, 7)):
-            pl.when(w == w0)(functools.partial(z_step, t))
-
-        @pl.when((w == 0))
-        def _():
-            y_first(1)
-
-        @pl.when((w == 1))
-        def _():
-            y_second(1)
-            y_third(1)
-
-        @pl.when((w == 3))
-        def _():
-            y_ready(1)
-
-        @pl.when((w >= 8) & (lax.rem(w, 2) == 0) & (w < items))
-        def _():
-            z_step(w // 2 + 4)
-
-        @pl.when((w >= 2) & (w < items + 2))
-        def _():
-            add_first(w - 2)
+    def item(w, _):
+        @pl.when((w >= LAG) & (w < items + LAG))
+        def _():
+            add_first(w - LAG)
 
         @pl.when(w < items)
         def _():
             multiply(w)
 
-        @pl.when((w >= 2) & (w < items + 2))
-        def _():
-            b_copy(w - 2).start()
+        @pl.when((w >= LAG) & (w < items + LAG))
+        def _():
+            b_copy(w - LAG).start()
 
         @pl.when(w < items)
         def _():
             a_copy(w).start()
             c_copy(w).start()
 
-        @pl.when(w >= 4)
-        def _():
-            finish(w - 4)
+        @pl.when(w >= 2 * LAG)
+        def _():
+            finish(w - 2 * LAG)
 
         return 0
 
-    lax.fori_loop(0, items + 4, body, 0)
+    def done(n):
+        early = lax.max(lax.min(lax.min(n - 13, (n - 10) // 2), 5), 0)
+        late = (lax.max(n - 20, 0) * 5) // 4
+        return lax.min(early + late, items - 2 + (2 * LAG + 2) * (n // 42))
+
+    sums[...] = jnp.zeros_like(sums)
+    for c in range(LEAD):
+        z_hop(1, c)
+    z_tick(0, 0)
+    y_own(0)
+    for n in range(1, 12):
+        z_tick(n, n % 2)
+        if n == 6:
+            y_first(0)
+        if n == 9:
+            y_second(0)
+
+    def tick(n, _):
+        pl.when(lax.rem(n, 2) == 0)(functools.partial(z_tick, n, 0))
+        pl.when(lax.rem(n, 2) == 1)(functools.partial(z_tick, n, 1))
+        for n0, f, g in ((12, y_third, 0), (14, y_ready, 0), (15, y_first, 1), (17, y_second, 1), (19, y_third, 1), (21, y_ready, 1)):
+            pl.when(n == n0)(functools.partial(f, g))
+        lax.fori_loop(done(n - 1), done(n), item, 0)
+        return 0
+
+    lax.fori_loop(12, 50, tick, 0)
 
     def n_copy(i, receiving):
         slot = at_r(r - i) if receiving else r
@@ -236,7 +245,8 @@
             src_ref=ref, dst_ref=ref, send_sem=n_send.at[i], recv_sem=n_recv.at[i],
             device_id=(x, at_r(r + i), z), device_id_type=MESH)
 
-    sums_all[r] = sums[...]
+    for g in range(GROUPS):
+        sums_all[r, :, gw * g : gw * (g + 1)] = jnp.sum(sums[g], axis=0, keepdims=True)
     for i in range(1, nr):
         n_copy(i, False).start()
 
@@ -269,9 +279,10 @@
     total = sums_all[0]
     for i in range(1, nr):
         total += sums_all[i]
-    scale = 1.0 / (jnp.sum(total, axis=1, keepdims=True) * (1.0 / (rows * nr)) + 1e-6)
+    scale = 1.0 / (total * (1.0 / (rows * nr)) + 1e-6)
     for g in range(GROUPS):
-        out[:, gw * g : gw * (g + 1)] = (sq[g] * scale[g]).astype(out.dtype)
+        cols = slice(gw * g, gw * (g + 1))
+        out[:, cols] = (sq[g] * scale[:, cols]).astype(out.dtype)
     for i in range(1, nr):
         n_copy(i, False).wait_send()
 
@@ -283,12 +294,15 @@
     items = CHUNKS * GROUPS
     dma = pltpu.SemaphoreType.DMA
     smem, vmem = pl.BlockSpec(memory_space=pltpu.SMEM), pl.BlockSpec(memory_space=pltpu.VMEM)
+    hbm = pl.BlockSpec(memory_space=pltpu.HBM)
     out = pl.pallas_call(
         functools.partial(kernel, nl, nr, nz),
         out_shape=jax.ShapeDtypeStruct((rows, tile), bf16),
-        in_specs=[smem, smem, vmem, vmem],
+        in_specs=[smem, smem, hbm, hbm],
         out_specs=vmem,
         scratch_shapes=[
+            pltpu.VMEM((rows, tile), bf16),
+            pltpu.VMEM(right_values.shape, bf16),
             pltpu.VMEM((nz, rows, tile), bf16),
             pltpu.VMEM((nr, GROUPS, tile, nl * gw), bf16),
             pltpu.VMEM((nl, GROUPS, rows, gw), f32),
@@ -297,13 +311,13 @@
             pltpu.VMEM((GROUPS, rows, gw), f32),
             pltpu.VMEM((GROUPS, rows, gw), f32),
             pltpu.VMEM((GROUPS, 8, gw), f32),
-            pltpu.VMEM((nr, GROUPS, 8, gw), f32),
+            pltpu.VMEM((nr, 1, tile), f32),
             dma((nz // 2, CHUNKS)), dma((nz // 2, CHUNKS)),
             dma((nz // 2, CHUNKS)), dma((nz // 2, CHUNKS)),
             dma((GROUPS, 2, 3)), dma((GROUPS, 2, 3)),
             dma((GROUPS, 2, 4)), dma((GROUPS, 2, 4)),
             dma((items,)), dma((items,)), dma((items,)), dma((items,)), dma((items,)), dma((items,)),
-            dma((nr,)), dma((nr,)),
+            dma((nr,)), dma((nr,)), dma((2,)),
         ],
         compiler_params=pltpu.CompilerParams(
             collective_id=0, has_side_effects=True, vmem_limit_bytes=40 * 1024 * 1024),

time: 91 us -> 84.4 us (0.927)
  Pallas kernels: 87.2 us -> 80.7 us
    pallas_call x1, Pallas kernels: 87.2 us -> 80.7 us  [per_device(): pl.pallas_call(functools.partial(kernel, nl, nr, nz), out_shape=jax.Shape...]
where the time goes in v3:
time: 84.4 us; the launch traced here: 84.3 us
  Pallas kernels  80.7 us (96%)
  local copies, waits for them, and re-layouts  3.55 us (4%)
    pallas_call x1, Pallas kernels, per_device(): pl.pallas_call(functools.partial(kernel, nl, nr, nz), out_shape=jax.Shape...  80.7 us
    unnamed x9, local copies, waits for them, and re-layouts  3.55 us

profile of v3, /device:TPU:1, one launch (start us, length us, event | category | flops | bytes accessed | tf_op | source)
XLA Modules:
  0.0 84.3 jit_solution(12094298955723581169)
XLA Ops:
  0.0 0.0 copy-start.2
  0.0 0.0 copy-start.3
  0.0 0.7 copy-done.2
  0.7 0.0 copy-done.3
  0.7 0.0 copy-start
  0.7 1.0 %copy-done = bf16[1024,1,256]{2,0,1:T(8,128)(2,1)S(1)} copy-done((bf16[1024,1,256]{2,0,1:T(8,128)(2,1)S(1)}, bf16[1024,1,256]{2,0,1:T(8,128)(2,1)}, u32[]{:S(2)}) %copy-start) | copy-done | bytes 524312
  1.7 0.0 copy-start.1
  1.7 1.0 %copy-done.1 = bf16[256,4,256]{2,1,0:T(4,128)(2,1)S(1)} copy-done((bf16[256,4,256]{2,1,0:T(4,128)(2,1)S(1)}, bf16[256,4,256]{2,1,0:T(4,128)(2,1)}, u32[]{:S(2)}) %copy-start.1) | copy-done | bytes 524312
  2.8 80.7 %shard_map.46 = bf16[1024,256]{1,0:T(8,128)(2,1)S(1)} custom-call(s32[4]{0:T(128)S(1)} %bitcast.6, s32[4]{0:T(128)S(1)} %bitcast.7, bf16[1024,256]{1,0:T(8,128)(2,1)S(1)} %bitcast.5, bf16[256,4,256]{2,1,0:T(4,128)(2,1)S(1)} %copy-done.1), custom_call_target="tpu_custom_call" | custom-call | tf_op jit(solution)/shard_map/pallas_call | solution.py:298
  83.5 0.8 copy.6
Async XLA Ops:
  0.0 0.7 copy-start.2
  0.0 0.7 copy-start.3
  0.7 1.0 %copy-start = (bf16[1024,1,256]{2,0,1:T(8,128)(2,1)S(1)}, bf16[1024,1,256]{2,0,1:T(8,128)(2,1)}, u32[]{:S(2)}) copy-start(bf16[1024,1,256]{2,0,1:T(8,128)(2,1)} %param.4) | copy-start | bytes 1572868
  1.7 1.0 %copy-start.1 = (bf16[256,4,256]{2,1,0:T(4,128)(2,1)S(1)}, bf16[256,4,256]{2,1,0:T(4,128)(2,1)}, u32[]{:S(2)}) copy-start(bf16[256,4,256]{2,1,0:T(4,128)(2,1)} %rv_hbm.1) | copy-start | bytes 1572868

commit v4 on v3

--- a/solution.py
+++ b/solution.py
@@ -10,7 +10,7 @@
 MESH = pl.DeviceIdType.MESH
 CHUNKS = 16
 LEAD = 1
-LAG = 4
+LAG = 6
 GROUPS = 2
 
 
@@ -50,11 +50,6 @@
     for i in range(rows // tile):
         block = lv[pl.ds(i * tile, tile), :].astype(jnp.float32) * lp[i].astype(jnp.float32)
         lbuf[z, pl.ds(i * tile, tile), :] = block.astype(lbuf.dtype)
-    fetch_right.wait()
-    for l in range(nl):
-        block = (rv[:, l, :].astype(jnp.float32) * rp[l].astype(jnp.float32)).astype(rbuf.dtype)
-        for g in range(GROUPS):
-            rbuf[r, g, :, gw * l : gw * (l + 1)] = block[:, gw * g : gw * (g + 1)]
     pl.semaphore_wait(barrier, len(peers))
 
     def z_copy(h, c, long, receiving):
@@ -87,7 +82,7 @@
                     z_hop(h, c)
             else:
                 c = (n - delay) // 2
-                pl.when(c < CHUNKS)(functools.partial(z_hop, h, c))
+                pl.when((c >= 0) & (c < CHUNKS))(functools.partial(z_hop, h, c))
 
     def y_copy(g, i, up, hop, receiving):
         d = 2 if up else -2
@@ -213,13 +208,18 @@
 
     def done(n):
         early = lax.max(lax.min(lax.min(n - 13, (n - 10) // 2), 5), 0)
-        late = (lax.max(n - 20, 0) * 5) // 4
+        late = (lax.max(n - 20, 0) * 5) // 4 + 3 * LAG * (n // 43)
         return lax.min(early + late, items - 2 + (2 * LAG + 2) * (n // 42))
 
     sums[...] = jnp.zeros_like(sums)
     for c in range(LEAD):
         z_hop(1, c)
     z_tick(0, 0)
+    fetch_right.wait()
+    for l in range(nl):
+        block = (rv[:, l, :].astype(jnp.float32) * rp[l].astype(jnp.float32)).astype(rbuf.dtype)
+        for g in range(GROUPS):
+            rbuf[r, g, :, gw * l : gw * (l + 1)] = block[:, gw * g : gw * (g + 1)]
     y_own(0)
     for n in range(1, 12):
         z_tick(n, n % 2)
@@ -320,7 +320,7 @@
             dma((nr,)), dma((nr,)), dma((2,)),
         ],
         compiler_params=pltpu.CompilerParams(
-            collective_id=0, has_side_effects=True, vmem_limit_bytes=40 * 1024 * 1024),
+            collective_id=0, has_side_effects=True, vmem_limit_bytes=66000000),
     )(left_pattern.reshape(-1), right_pattern.reshape(-1), left_values.reshape(rows, tile), right_values)
     return out.reshape(rows, 1, tile)
 

time: 84.4 us -> 82.3 us (0.975)
  local copies, waits for them, and re-layouts: 3.55 us -> 1.87 us
    unnamed x9 -> x1, local copies, waits for them, and re-layouts: 3.55 us -> 1.87 us
where the time goes in v4:
time: 82.3 us; the launch traced here: 82.1 us
  Pallas kernels  80.2 us (97%)
  local copies, waits for them, and re-layouts  1.87 us (2%)
    pallas_call x1, Pallas kernels, per_device(): pl.pallas_call(functools.partial(kernel, nl, nr, nz), out_shape=jax.Shape...  80.2 us
    unnamed x1, local copies, waits for them, and re-layouts  1.87 us

profile of v4, /device:TPU:1, one launch (start us, length us, event | category | flops | bytes accessed | tf_op | source)
XLA Modules:
  0.0 82.1 jit_solution(16035662954116310499)
XLA Ops:
  0.0 80.2 %shard_map.46 = bf16[1024,256]{1,0:T(8,128)(2,1)} custom-call(s32[4]{0:T(128)} %bitcast.6, s32[4]{0:T(128)} %bitcast.7, bf16[1024,256]{1,0:T(8,128)(2,1)} %bitcast.5, bf16[256,4,256]{2,1,0:T(4,128)(2,1)} %rv_hbm.1), custom_call_target="tpu_custom_call" | custom-call | tf_op jit(solution)/shard_map/pallas_call | solution.py:298
  80.3 1.9 %copy.6 = bf16[1024,1,256]{2,0,1:T(8,128)(2,1)} copy(bf16[1024,1,256]{2,0,1:T(8,128)(2,1)} %bitcast.4) | data formatting | bytes 1048576

commit v5 on v4

--- a/solution.py
+++ b/solution.py
@@ -183,22 +183,16 @@
         sums[g] += jnp.sum(square.reshape(cr // 8, 8, gw), axis=0)
 
     def item(w, _):
+        @pl.when(w < items)
+        def _():
+            multiply(w)
+            a_copy(w).start()
+            c_copy(w).start()
+
         @pl.when((w >= LAG) & (w < items + LAG))
         def _():
             add_first(w - LAG)
-
-        @pl.when(w < items)
-        def _():
-            multiply(w)
-
-        @pl.when((w >= LAG) & (w < items + LAG))
-        def _():
             b_copy(w - LAG).start()
-
-        @pl.when(w < items)
-        def _():
-            a_copy(w).start()
-            c_copy(w).start()
 
         @pl.when(w >= 2 * LAG)
         def _():

time: 82.3 us -> 82 us (level)
  no operation moved by 1% of the time
where the time goes in v5:
time: 82 us; the launch traced here: 81.9 us
  Pallas kernels  80 us (98%)
  local copies, waits for them, and re-layouts  1.87 us (2%)
    pallas_call x1, Pallas kernels, per_device(): pl.pallas_call(functools.partial(kernel, nl, nr, nz), out_shape=jax.Shape...  80 us
    unnamed x1, local copies, waits for them, and re-layouts  1.87 us

profile of v5, /device:TPU:1, one launch (start us, length us, event | category | flops | bytes accessed | tf_op | source)
XLA Modules:
  0.0 81.9 jit_solution(4250526609765843275)
XLA Ops:
  0.0 80.0 %shard_map.46 = bf16[1024,256]{1,0:T(8,128)(2,1)} custom-call(s32[4]{0:T(128)} %bitcast.6, s32[4]{0:T(128)} %bitcast.7, bf16[1024,256]{1,0:T(8,128)(2,1)} %bitcast.5, bf16[256,4,256]{2,1,0:T(4,128)(2,1)} %rv_hbm.1), custom_call_target="tpu_custom_call" | custom-call | tf_op jit(solution)/shard_map/pallas_call | solution.py:292
  80.0 1.9 %copy.6 = bf16[1024,1,256]{2,0,1:T(8,128)(2,1)} copy(bf16[1024,1,256]{2,0,1:T(8,128)(2,1)} %bitcast.4) | data formatting | bytes 1048576
